TPU v7x, 512 devices: a whole 4x8x8 slice. The times are simulated.
512 devices in a mesh: dp: 8 (over x, core), context: 64 (over y, z).
Axes of the slice: x: 4, y: 8, z: 8, core: 2. Of those that a mesh axis runs over, the one named last changes fastest.
Arguments:
- queries: bfloat16 [8, 8192, 2048], P('dp', 'context'), may hold values from -6 to 6
- key_rows: bfloat16 [8, 8192, 2048], P('dp', 'context'), may hold values from -6 to 6
- value_rows: bfloat16 [8, 8192, 2048], P('dp', 'context'), may hold values from -6 to 6
- out_grad: bfloat16 [8, 8192, 2048], P('dp', 'context'), may hold values from -6 to 6
- feature_maps: bfloat16 [16, 128, 128], replicated, may hold values from -0.5 to 0.5
Outputs:
- query_grad: bfloat16 [8, 8192, 2048], P('dp', 'context')
- key_grad: bfloat16 [8, 8192, 2048], P('dp', 'context')
- value_grad: bfloat16 [8, 8192, 2048], P('dp', 'context')
- maps_grad: float32 [2048, 128], P(('dp', 'context'))
All inputs are finite; a program needn't handle non-finite values.
Results may differ from a plain program's by a relative error of at most 0.0085.
Values sent between devices are 32-bit elements; how exact they have to be, the bound alone decides.
A program may use at most 64 MiB of HBM per device.

v0:
```python
import math

import jax
import jax.numpy as jnp
from jax import lax
from jax.sharding import PartitionSpec as P


def block_sums(kv_all, grad_all):
    running_kv = jnp.cumsum(kv_all, axis=0)
    running_grad = jnp.cumsum(grad_all, axis=0)
    before = running_kv - kv_all
    after = running_grad[-1:] - running_grad
    return (before, after)


def split_state(state):
    upper = state.astype(jnp.bfloat16)
    lower = (state - upper.astype(jnp.float32)).astype(jnp.bfloat16)
    return (upper, lower)


def state_product(form, rows, parts):
    return jnp.einsum(form, rows, parts[0], preferred_element_type=jnp.float32) + jnp.einsum(
        form, rows, parts[1], preferred_element_type=jnp.float32
    )


def per_device(queries, key_rows, value_rows, out_grad, feature_maps):
    tokens = queries.shape[1]
    head_count = feature_maps.shape[0]
    head_width = feature_maps.shape[1]
    ranks = lax.axis_size("context")
    length = tokens * ranks
    factor = 1.0 / math.sqrt(head_width * length)
    norm_factor = 1.0 / math.sqrt(lax.axis_size("dp") * length)
    query_heads = queries.reshape(tokens, head_count, head_width)
    key_heads = key_rows.reshape(tokens, head_count, head_width)
    value_heads = value_rows.reshape(tokens, head_count, head_width)
    grad_heads = out_grad.reshape(tokens, head_count, head_width)
    feat_query = jnp.einsum(
        "thd,hde->hte", query_heads, feature_maps, preferred_element_type=jnp.float32
    ).astype(jnp.bfloat16)
    feat_key = jnp.einsum(
        "thd,hde->hte", key_heads, feature_maps, preferred_element_type=jnp.float32
    ).astype(jnp.bfloat16)
    kv_local = jnp.einsum("hsd,she->hde", feat_key, value_heads, preferred_element_type=jnp.float32)
    grad_local = jnp.einsum(
        "htd,the->hde", feat_query, grad_heads, preferred_element_type=jnp.float32
    )
    state_rows = head_count * head_width
    group_rows = state_rows // ranks
    kv_groups = kv_local.reshape(ranks, group_rows, head_width)
    grad_groups = grad_local.reshape(ranks, group_rows, head_width)
    kv_all, grad_all = (
        lax.all_to_all(kv_groups, "context", split_axis=0, concat_axis=0, tiled=True),
        lax.all_to_all(grad_groups, "context", split_axis=0, concat_axis=0, tiled=True),
    )
    before, after = block_sums(kv_all, grad_all)
    before_mine, after_mine = (
        lax.all_to_all(before, "context", split_axis=0, concat_axis=0, tiled=True),
        lax.all_to_all(after, "context", split_axis=0, concat_axis=0, tiled=True),
    )
    prefix_parts = split_state(before_mine.reshape(head_count, head_width, head_width))
    suffix_parts = split_state(after_mine.reshape(head_count, head_width, head_width))
    causal = jnp.arange(tokens)[:, None] >= jnp.arange(tokens)[None, :]
    score_ab = jnp.where(
        causal,
        jnp.einsum("htd,hsd->hts", feat_query, feat_key, preferred_element_type=jnp.float32),
        0.0,
    ).astype(jnp.bfloat16)
    score_gv = jnp.where(
        causal,
        jnp.einsum("the,she->hts", grad_heads, value_heads, preferred_element_type=jnp.float32),
        0.0,
    ).astype(jnp.bfloat16)
    feat_qgrad = factor * (
        jnp.einsum("hts,hsd->htd", score_gv, feat_key, preferred_element_type=jnp.float32)
        + state_product("the,hde->htd", grad_heads, prefix_parts)
    )
    feat_qgrad = feat_qgrad.astype(jnp.bfloat16)
    query_grad = jnp.einsum(
        "hte,hde->thd", feat_qgrad, feature_maps, preferred_element_type=jnp.float32
    )
    query_grad = query_grad.astype(jnp.bfloat16).reshape(1, tokens, head_count * head_width)
    query_term = jnp.einsum(
        "thd,hte->hde", query_heads, feat_qgrad, preferred_element_type=jnp.float32
    )
    feat_kgrad = factor * (
        jnp.einsum("hts,htd->hsd", score_gv, feat_query, preferred_element_type=jnp.float32)
        + state_product("she,hde->hsd", value_heads, suffix_parts)
    )
    feat_kgrad = feat_kgrad.astype(jnp.bfloat16)
    value_grad = factor * (
        jnp.einsum("hts,the->she", score_ab, grad_heads, preferred_element_type=jnp.float32)
        + state_product("hsd,hde->she", feat_key, suffix_parts)
    )
    value_grad = value_grad.astype(jnp.bfloat16).reshape(1, tokens, head_count * head_width)
    key_grad = jnp.einsum(
        "hse,hde->shd", feat_kgrad, feature_maps, preferred_element_type=jnp.float32
    )
    key_grad = key_grad.astype(jnp.bfloat16).reshape(1, tokens, head_count * head_width)
    key_term = jnp.einsum("shd,hse->hde", key_heads, feat_kgrad, preferred_element_type=jnp.float32)
    both_terms = (query_term + key_term).reshape(state_rows, head_width)
    maps_grad = (
        lax.psum_scatter(both_terms, ("dp", "context"), scatter_dimension=0, tiled=True)
        * norm_factor
    )
    return (query_grad, key_grad, value_grad, maps_grad)


def solution(mesh):
    in_specs = (
        P("dp", "context", None),
        P("dp", "context", None),
        P("dp", "context", None),
        P("dp", "context", None),
        P(),
    )
    out_specs = (
        P("dp", "context", None),
        P("dp", "context", None),
        P("dp", "context", None),
        P(("dp", "context"), None),
    )
    return jax.shard_map(
        per_device, mesh=mesh, in_specs=in_specs, out_specs=out_specs, check_vma=False
    )
```

profile of v0, /device:TPU:1, one launch (start us, length us, event | category | flops | bytes accessed | tf_op | source)
XLA Modules:
  0.0 450.5 jit_solution(7559879795493648647)
XLA Ops:
  7.2 1.4 copy.69
  8.6 0.1 copy.71
  8.7 0.7 copy-done.3
  9.4 0.3 convolution_convert_fusion.3
  9.8 1.3 fusion.21
  11.1 17.1 %all-to-all-start = ((f32[64,32,128]{2,1,0:T(8,128)}), f32[64,32,128]{2,1,0:T(8,128)S(1)}, u32[]{:S(2)}, u32[]{:S(2)}) async-start(f32[64,32,128]{2,1,0:T(8,128)} %bitcast.110), calls=%async_computation | async-start | bytes 2097152 | tf_op jit(solution)/shard_map/all_to_all | solution.py:56
  28.2 1.3 copy.68
  29.5 2.0 copy.70
  31.6 1.4 convolution_convert_fusion.1
  33.0 0.8 copy-done.1
  33.8 1.5 fusion.30
  35.3 19.8 %all-to-all-done = f32[64,32,128]{2,1,0:T(8,128)S(1)} async-done(((f32[64,32,128]{2,1,0:T(8,128)}), f32[64,32,128]{2,1,0:T(8,128)S(1)}, u32[]{:S(2)}, u32[]{:S(2)}) %all-to-all-start) | async-done | bytes 1048608 | tf_op jit(solution)/shard_map/all_to_all | solution.py:56
  55.1 9.1 %all-to-all-start.2 = ((f32[64,32,128]{2,1,0:T(8,128)}), f32[64,32,128]{2,1,0:T(8,128)}, u32[]{:S(2)}, u32[]{:S(2)}) async-start(f32[64,32,128]{2,1,0:T(8,128)} %bitcast.109), calls=%async_computation.2 | async-start | bytes 2097152 | tf_op jit(solution)/shard_map/all_to_all | solution.py:57
  64.2 6.6 %fusion.25 = f32[64,32,128]{2,1,0:T(8,128)S(1)} fusion(f32[64,32,128]{2,1,0:T(8,128)S(1)} %all-to-all-done), kind=kOutput, calls=%fused_computation.44 | output fusion | flops 16515072 | bytes 2097152 | tf_op jit(solution)/shard_map/jit(cumsum)/reduce_window_sum | solution.py:10
  70.8 1.2 sub.19
  72.0 18.6 %all-to-all-done.2 = f32[64,32,128]{2,1,0:T(8,128)} async-done(((f32[64,32,128]{2,1,0:T(8,128)}), f32[64,32,128]{2,1,0:T(8,128)}, u32[]{:S(2)}, u32[]{:S(2)}) %all-to-all-start.2) | async-done | bytes 1048608 | tf_op jit(solution)/shard_map/all_to_all | solution.py:57
  90.6 9.5 %all-to-all-start.1 = ((f32[64,32,128]{2,1,0:T(8,128)}), f32[64,32,128]{2,1,0:T(8,128)}, u32[]{:S(2)}, u32[]{:S(2)}) async-start(f32[64,32,128]{2,1,0:T(8,128)} %sub.19), calls=%async_computation.1 | async-start | bytes 2097152 | tf_op jit(solution)/shard_map/all_to_all | solution.py:61
  100.2 1.3 fusion.26
  101.5 1.1 broadcast_subtract_fusion
  102.5 24.1 %all-to-all-done.1 = f32[64,32,128]{2,1,0:T(8,128)} async-done(((f32[64,32,128]{2,1,0:T(8,128)}), f32[64,32,128]{2,1,0:T(8,128)}, u32[]{:S(2)}, u32[]{:S(2)}) %all-to-all-start.1) | async-done | bytes 1048608 | tf_op jit(solution)/shard_map/all_to_all | solution.py:61
  126.7 9.4 %all-to-all-start.3 = ((f32[64,32,128]{2,1,0:T(8,128)}), f32[64,32,128]{2,1,0:T(8,128)}, u32[]{:S(2)}, u32[]{:S(2)}) async-start(f32[64,32,128]{2,1,0:T(8,128)} %broadcast_subtract_fusion), calls=%async_computation.3 | async-start | bytes 2097152 | tf_op jit(solution)/shard_map/all_to_all | solution.py:62
  136.1 0.2 all-reduce.3.cloned.1.call-start
  136.3 0.5 fusion.10
  136.8 0.3 fusion.27
  137.1 0.7 copy-done.2
  137.9 1.3 fusion.29
  139.2 1.7 fusion.15
  140.9 0.5 fusion.28
  141.4 0.5 fusion.12
  142.0 1.3 convolution_convert_fusion.2
  143.2 1.3 fusion.32
  144.5 18.0 %all-to-all-done.3 = f32[64,32,128]{2,1,0:T(8,128)} async-done(((f32[64,32,128]{2,1,0:T(8,128)}), f32[64,32,128]{2,1,0:T(8,128)}, u32[]{:S(2)}, u32[]{:S(2)}) %all-to-all-start.3) | async-done | bytes 1048608 | tf_op jit(solution)/shard_map/all_to_all | solution.py:62
  162.5 1.7 fusion.14
  164.3 0.5 fusion.19
  164.8 1.5 fusion.31
  166.3 0.5 fusion.13
  166.7 0.5 copy-done.4
  167.3 0.3 copy-done.9
  167.6 1.3 convolution_add_fusion
  168.9 0.0 all-reduce.3.cloned.1.call-update
  169.0 2.1 copy.56
  171.1 2.7 fusion.2
  173.8 1.9 fusion.9
  175.7 1.0 copy.58
  176.7 0.5 convolution_convert_fusion
  177.2 1.0 copy.57
  178.2 264.2 %all-reduce.3.cloned.1.call-done = f32[2048,128]{1,0:T(8,128)} async-done(((f32[2048,128]{1,0:T(8,128)}), f32[2048,128]{1,0:T(8,128)}) %all-reduce.3.cloned.1.call-update) | async-done | bytes 1048592
  442.4 1.3 dynamic-slice_multiply_fusion
  (19 shorter events, 0.1 us)
Async XLA Ops:
  7.2 2.2 copy-start
  7.2 1.4 copy-start.10
  8.6 0.8 copy-start.3
  11.1 44.0 %all-to-all-start = ((f32[64,32,128]{2,1,0:T(8,128)}), f32[64,32,128]{2,1,0:T(8,128)S(1)}, u32[]{:S(2)}, u32[]{:S(2)}) async-start(f32[64,32,128]{2,1,0:T(8,128)} %bitcast.110), calls=%async_computation | async-start | bytes 2097152 | tf_op jit(solution)/shard_map/all_to_all | solution.py:56
  33.0 0.8 copy-start.1
  55.1 35.6 %all-to-all-start.2 = ((f32[64,32,128]{2,1,0:T(8,128)}), f32[64,32,128]{2,1,0:T(8,128)}, u32[]{:S(2)}, u32[]{:S(2)}) async-start(f32[64,32,128]{2,1,0:T(8,128)} %bitcast.109), calls=%async_computation.2 | async-start | bytes 2097152 | tf_op jit(solution)/shard_map/all_to_all | solution.py:57
  90.6 36.0 %all-to-all-start.1 = ((f32[64,32,128]{2,1,0:T(8,128)}), f32[64,32,128]{2,1,0:T(8,128)}, u32[]{:S(2)}, u32[]{:S(2)}) async-start(f32[64,32,128]{2,1,0:T(8,128)} %sub.19), calls=%async_computation.1 | async-start | bytes 2097152 | tf_op jit(solution)/shard_map/all_to_all | solution.py:61
  126.7 35.9 %all-to-all-start.3 = ((f32[64,32,128]{2,1,0:T(8,128)}), f32[64,32,128]{2,1,0:T(8,128)}, u32[]{:S(2)}, u32[]{:S(2)}) async-start(f32[64,32,128]{2,1,0:T(8,128)} %broadcast_subtract_fusion), calls=%async_computation.3 | async-start | bytes 2097152 | tf_op jit(solution)/shard_map/all_to_all | solution.py:62
  136.1 306.3 %all-reduce.3.cloned.1.call-start = ((), (), s32[]{:S(2)}) async-start(), calls=%async_computation.4 | async-start | bytes 2097152
  136.8 1.0 copy-start.2
  142.0 1.3 copy-start.5
  164.2 2.0 copy-start.6
  164.7 1.5 copy-start.8
  166.2 1.0 copy-start.4
  166.2 1.4 copy-start.9
  169.0 2.1 copy-start.7
Sparse Core Ops, SparseCore 0:
  169.1 273.2 all-reduce.2
where the time goes:
time: 452 us; the launch traced here: 450 us
  waiting for transfers between devices  345 us (76%)
  starting transfers between devices  45.3 us (10%)
  matrix products  19.1 us (4%)
  other arithmetic  14.9 us (3%)
  between operations  14.3 us (3%)
  local copies, waits for them, and re-layouts  12.1 us (3%)
    unnamed x2, waiting for transfers between devices  264 us
    all_to_all x1, waiting for transfers between devices, per_device(): lax.all_to_all(before, 'context', split_axis=0, concat_axis=0, tiled=True)  24.1 us
    all_to_all x1, waiting for transfers between devices, per_device(): lax.all_to_all(kv_groups, 'context', split_axis=0, concat_axis=0, tiled=T...  19.8 us
    all_to_all x1, waiting for transfers between devices, per_device(): lax.all_to_all(grad_groups, 'context', split_axis=0, concat_axis=0, tiled...  18.6 us
    all_to_all x1, waiting for transfers between devices, per_device(): lax.all_to_all(after, 'context', split_axis=0, concat_axis=0, tiled=True)  18 us
    all_to_all x1, starting transfers between devices, per_device(): lax.all_to_all(kv_groups, 'context', split_axis=0, concat_axis=0, tiled=T...  17.1 us
    all_to_all x1, starting transfers between devices, per_device(): lax.all_to_all(before, 'context', split_axis=0, concat_axis=0, tiled=True)  9.48 us
    all_to_all x1, starting transfers between devices, per_device(): lax.all_to_all(after, 'context', split_axis=0, concat_axis=0, tiled=True)  9.4 us
  transfers between devices with their start and end apart: 5, of which 5 were waited for; matrix products, arithmetic and copies ran while one was open for 7% of the time, Pallas kernels for 0%

commit v1 on v0

v1 whole, which is shorter than its diff:
```python
import functools
import math

import jax
import jax.numpy as jnp
from jax import lax
from jax.experimental import pallas as pl
from jax.experimental.pallas import tpu as pltpu
from jax.sharding import PartitionSpec as P

F32, BF16 = jnp.float32, jnp.bfloat16
PIECES = 2


def nn(a, b):
    return lax.dot_general(a, b, (((1,), (0,)), ((), ())), preferred_element_type=F32)


def nt(a, b):
    return lax.dot_general(a, b, (((1,), (1,)), ((), ())), preferred_element_type=F32)


def tn(a, b):
    return lax.dot_general(a, b, (((0,), (0,)), ((), ())), preferred_element_type=F32)


def split(state):
    upper = state.astype(BF16)
    return upper, (state - upper.astype(F32)).astype(BF16)


def body(sizes, q_ref, k_ref, v_ref, g_ref, f_ref, qg_ref, kg_ref, vg_ref, mg_ref,
         a_s, b_s, state, part, base, lda, ldb, lvg, maps, peer, colbuf, rowsum, rowout, rowbuf,
         part_sem, base_sem, peer_sem, col_sem, row_sem, part_out, base_out, scan_out, peer_out, col_out, row_out):
    ndp, ny, nz, factor, norm = sizes
    tokens, width = q_ref.shape[1], f_ref.shape[1]
    unit = 2 * width
    piece = unit // PIECES
    steps, right, left = nz - 1, nz // 2, nz // 2 - 1
    per_owner = nz // ndp
    blocks = ny * nz
    d = lax.axis_index("dp")
    n = lax.axis_index("context")
    y, z = n // nz, lax.rem(n, nz)

    def at(dp, block):
        return dict(device_id=(dp, block), device_id_type=pl.DeviceIdType.MESH)

    def along(t, hops):
        return lax.rem(n + (1 - 2 * t) * hops + blocks, blocks)

    def order(t):
        return jnp.where(t == 0, n, blocks - 1 - n)

    def pair_of(r):
        return lax.rem(z + r + d * per_owner, nz)

    def rows_of(q):
        return pl.ds(q * piece, piece)

    barrier = pltpu.get_barrier_semaphore()
    for hop in (1, blocks - 1):
        pl.semaphore_signal(barrier, inc=1, **at(d, lax.rem(n + hop, blocks)))
    for i in range(1, ny):
        pl.semaphore_signal(barrier, inc=1, **at(d, lax.rem(y + i, ny) * nz + z))
    for i in range(1, nz):
        pl.semaphore_signal(barrier, inc=1, **at(d, y * nz + lax.rem(z + i, nz)))
    for i in range(1, ndp):
        pl.semaphore_signal(barrier, inc=1, **at(lax.rem(d + i, ndp), n))

    def cols(h):
        return pl.ds(pl.multiple_of(h * width, width), width)

    def head_rows(hh):
        return pl.ds(pl.multiple_of(hh * width, width), width)

    def features(i, carry):
        m, hh = i // 2, lax.rem(i, 2)
        r = jnp.where(m == nz - 1, 0, jnp.where(lax.rem(m, 2) == 0, nz - 1 - m // 2, 1 + m // 2))
        p = pair_of(r)
        h = 2 * p + hh
        fm = f_ref[h]
        a = nn(q_ref[0, :, cols(h)], fm).astype(BF16)
        b = nn(k_ref[0, :, cols(h)], fm).astype(BF16)
        a_s[h] = a
        b_s[h] = b
        state[0, p, head_rows(hh)] = tn(b, v_ref[0, :, cols(h)])
        state[1, p, head_rows(hh)] = tn(a, g_ref[0, :, cols(h)])
        return carry

    def inside(h, carry):
        causal = (lax.broadcasted_iota(jnp.int32, (tokens, tokens), 0)
                  >= lax.broadcasted_iota(jnp.int32, (tokens, tokens), 1))
        a, b = a_s[h], b_s[h]
        v, g = v_ref[0, :, cols(h)], g_ref[0, :, cols(h)]
        sab = jnp.where(causal, nt(a, b), 0.0).astype(BF16)
        sgv = jnp.where(causal, nt(g, v), 0.0).astype(BF16)
        lda[h] = nn(sgv, b)
        ldb[h] = tn(sgv, a)
        lvg[h] = tn(sab, g)
        return carry

    def part_copy(t, s, q, src):
        return pltpu.make_async_remote_copy(
            src_ref=src, dst_ref=part.at[t, s, rows_of(q)], send_sem=part_out.at[t],
            recv_sem=part_sem.at[t, s, q], **at(d, along(t, 1)))

    def base_copy(t, j, q, src, target, sem):
        return pltpu.make_async_remote_copy(
            src_ref=src, dst_ref=base.at[t, j, rows_of(q)], send_sem=sem.at[t],
            recv_sem=base_sem.at[t, j, q], **at(d, target))

    def base_wait(t, j, q):
        base_copy(t, j, q, base.at[t, j, rows_of(q)], n, base_out).wait_recv()

    lax.fori_loop(0, 4, features, 0)
    pl.semaphore_wait(barrier, 2 + (ny - 1) + (nz - 1) + (ndp - 1))
    for t in range(2):
        r = nz - 1 if t == 0 else 1
        for q in range(PIECES):
            part_copy(t, 0, q, state.at[t, pair_of(r), rows_of(q)]).start()

    def chain(s, carry):
        @pl.when(s <= nz // 2 - 1)
        def _():
            lax.fori_loop(4 * s, 4 * s + 4, features, 0)

        @pl.when(s >= nz // 2)
        def _():
            lax.fori_loop(4 * (s - nz // 2), 4 * (s - nz // 2) + 4, inside, 0)

        for q in range(PIECES):
            for t in range(2):
                p = pair_of(nz - 1 - s if t == 0 else lax.rem(1 + s, nz))
                part_copy(t, s - 1, q, part.at[t, s - 1, rows_of(q)]).wait_recv()

                @pl.when(order(t) > 0)
                def _(t=t, p=p, q=q):
                    state[t, p, rows_of(q)] += part[t, s - 1, rows_of(q)]

                @pl.when(s < steps)
                def _(t=t, p=p, q=q):
                    part_copy(t, s, q, state.at[t, p, rows_of(q)]).start()
        return carry

    lax.fori_loop(1, steps + 1, chain, 0)

    own = pair_of(0)

    def scan(i, carry):
        t = jnp.where(y < ny // 2, i, 1 - i)
        row = jnp.where(t == 0, y, ny - 1 - y)
        for q in range(PIECES):
            mine = state.at[t, own, rows_of(q)]

            @pl.when(row > 0)
            def _(q=q):
                base_wait(t, nz - 1, q)
                state[t, own, rows_of(q)] += base[t, nz - 1, rows_of(q)]

            base_copy(t, nz - 1, q, mine, along(t, nz), scan_out).start()
            base_copy(t, 0, q, mine, along(t, 1), base_out).start()

            @pl.when(row > 0)
            def _(q=q):
                base_copy(t, nz - 2, q, base.at[t, nz - 1, rows_of(q)], along(t, -1), base_out).start()
        return carry

    lax.fori_loop(0, 2, scan, 0)

    def scan_end(i, carry):
        row = jnp.where(i == 0, y, ny - 1 - y)

        @pl.when(row == 0)
        def _():
            for q in range(PIECES):
                base_wait(i, nz - 1, q)
                base_copy(i, nz - 2, q, base.at[i, nz - 1, rows_of(q)], along(i, -1), base_out).start()
        return carry

    def state_of(t, j, hh):
        from_base = jnp.where(order(t) >= j, base[t, j - 1, head_rows(hh)], 0.0)
        has_part = jnp.logical_and(order(t) > 0, j >= 2)
        slot = jnp.maximum(j - 2, 0)
        return from_base + jnp.where(has_part, part[t, slot, head_rows(hh)], 0.0)

    def finish_pair(r):
        p = pair_of(r)

        def finish(hh, carry):
            h = 2 * p + hh
            q, k = q_ref[0, :, cols(h)], k_ref[0, :, cols(h)]
            v, g = v_ref[0, :, cols(h)], g_ref[0, :, cols(h)]
            fm = f_ref[h]
            pu, plow = split(state_of(0, nz - r, hh))
            su, sl = split(state_of(1, jnp.where(r == 0, nz, r), hh))
            da = (factor * (lda[h] + (nt(g, pu) + nt(g, plow)))).astype(BF16)
            db = (factor * (ldb[h] + (nt(v, su) + nt(v, sl)))).astype(BF16)
            b = b_s[h]
            vg_ref[0, :, cols(h)] = (factor * (lvg[h] + (nn(b, su) + nn(b, sl)))).astype(BF16)
            qg_ref[0, :, cols(h)] = nt(da, fm).astype(BF16)
            kg_ref[0, :, cols(h)] = nt(db, fm).astype(BF16)
            maps[p, head_rows(hh)] = tn(q, da) + tn(k, db)
            return carry

        lax.fori_loop(0, 2, finish, 0)
        owner, place = p // per_owner, lax.rem(p, per_owner)

        @pl.when(owner != d)
        def _():
            pltpu.make_async_remote_copy(
                src_ref=maps.at[p], dst_ref=peer.at[place, d], send_sem=peer_out,
                recv_sem=peer_sem.at[place, d], **at(owner, n)).start()

    lax.fori_loop(0, 2, scan_end, 0)
    finish_pair(0)

    def spread(hop, carry):
        for q in range(PIECES):
            for t in range(2):
                base_wait(t, hop - 1, q)
                base_copy(t, hop, q, base.at[t, hop - 1, rows_of(q)], along(t, 1), base_out).start()
                base_wait(t, nz - 1 - hop, q)

                @pl.when(hop < left)
                def _(t=t, q=q):
                    base_copy(t, nz - 2 - hop, q, base.at[t, nz - 1 - hop, rows_of(q)], along(t, -1), base_out).start()

        lax.fori_loop(0, 2, lambda i, c: (finish_pair(jnp.where(i == 0, nz - hop, hop)), c)[1], 0)
        return carry

    lax.fori_loop(1, left + 1, spread, 0)
    for t in range(2):
        for q in range(PIECES):
            base_wait(t, right - 1, q)
    finish_pair(jnp.int32(nz // 2))

    for place in range(per_owner):
        mine = pl.ds(place * unit, unit)
        rowsum[mine] = maps[d * per_owner + place]
        for i in range(1, ndp):
            source = lax.rem(d + i, ndp)
            pltpu.make_async_remote_copy(
                src_ref=maps.at[0], dst_ref=peer.at[place, source], send_sem=peer_out,
                recv_sem=peer_sem.at[place, source], **at(source, n)).wait_recv()
            rowsum[mine] += peer[place, source]
    group = rowsum.shape[0] // ny
    mine = pl.ds(pl.multiple_of(y * group, group), group)
    for i in range(1, ny):
        there = lax.rem(y + i, ny)
        pltpu.make_async_remote_copy(
            src_ref=rowsum.at[pl.ds(pl.multiple_of(there * group, group), group)], dst_ref=colbuf.at[i], send_sem=col_out,
            recv_sem=col_sem.at[i], **at(d, there * nz + z)).start()
    total = rowsum[mine]
    for i in range(1, ny):
        pltpu.make_async_remote_copy(
            src_ref=colbuf.at[i], dst_ref=colbuf.at[i], send_sem=col_out,
            recv_sem=col_sem.at[i], **at(d, n)).wait_recv()
        total = total + colbuf[i]
    small = group // nz
    for i in range(nz):
        rowout[i] = total[i * small:(i + 1) * small]
    for i in range(1, nz):
        there = lax.rem(z + i, nz)
        pltpu.make_async_remote_copy(
            src_ref=rowout.at[there], dst_ref=rowbuf.at[i], send_sem=row_out,
            recv_sem=row_sem.at[i], **at(d, y * nz + there)).start()
    last = rowout[z]
    for i in range(1, nz):
        pltpu.make_async_remote_copy(
            src_ref=rowbuf.at[i], dst_ref=rowbuf.at[i], send_sem=row_out,
            recv_sem=row_sem.at[i], **at(d, n)).wait_recv()
        last = last + rowbuf[i]
    mg_ref[...] = last * norm

    def sent(ref, sem):
        pltpu.make_async_remote_copy(src_ref=ref, dst_ref=ref, send_sem=sem, recv_sem=row_sem.at[0], **at(d, n)).wait_send()

    for t in range(2):
        sent(part.at[t], part_out.at[t])
        sent(part.at[t], base_out.at[t])
        sent(state.at[t, 0], scan_out.at[t])
    sent(maps.at[pl.ds(0, nz - per_owner)], peer_out)
    sent(colbuf.at[pl.ds(1, ny - 1)], col_out)
    sent(rowbuf.at[pl.ds(1, nz - 1)], row_out)


def build(mesh, ny, nz):
    ndp = mesh.shape["dp"]

    def per_device(queries, key_rows, value_rows, out_grad, feature_maps):
        tokens = queries.shape[1]
        heads, width, _ = feature_maps.shape
        unit = 2 * width
        assert heads == 2 * nz and nz % ndp == 0 and ny * nz == mesh.shape["context"]
        per_owner = nz // ndp
        owned = per_owner * unit
        group = owned // ny
        small = group // nz
        length = tokens * ny * nz
        sizes = (ndp, ny, nz, 1.0 / math.sqrt(width * length), 1.0 / math.sqrt(ndp * length))
        dma = pltpu.SemaphoreType.DMA
        rows = jax.ShapeDtypeStruct(queries.shape, BF16)
        return pl.pallas_call(
            functools.partial(body, sizes),
            out_shape=(rows, rows, rows, jax.ShapeDtypeStruct((small, width), F32)),
            in_specs=[pl.BlockSpec(memory_space=pltpu.VMEM)] * 5,
            out_specs=(pl.BlockSpec(memory_space=pltpu.VMEM),) * 4,
            scratch_shapes=[
                pltpu.VMEM((heads, tokens, width), BF16),
                pltpu.VMEM((heads, tokens, width), BF16),
                pltpu.VMEM((2, nz, unit, width), F32),
                pltpu.VMEM((2, nz - 1, unit, width), F32),
                pltpu.VMEM((2, nz, unit, width), F32),
                pltpu.VMEM((heads, tokens, width), F32),
                pltpu.VMEM((heads, tokens, width), F32),
                pltpu.VMEM((heads, tokens, width), F32),
                pltpu.VMEM((nz, unit, width), F32),
                pltpu.VMEM((per_owner, ndp, unit, width), F32),
                pltpu.VMEM((ny, group, width), F32),
                pltpu.VMEM((owned, width), F32),
                pltpu.VMEM((nz, small, width), F32),
                pltpu.VMEM((nz, small, width), F32),
                dma((2, nz - 1, PIECES)),
                dma((2, nz, PIECES)),
                dma((per_owner, ndp)),
                dma((ny,)),
                dma((nz,)),
                dma((2,)),
                dma((2,)),
                dma((2,)),
                dma(()),
                dma(()),
                dma(()),
            ],
            compiler_params=pltpu.CompilerParams(
                collective_id=0, has_side_effects=True, vmem_limit_bytes=48 * 1024 * 1024),
        )(queries, key_rows, value_rows, out_grad, feature_maps)

    tokens_spec = P("dp", "context", None)
    return jax.shard_map(
        per_device, mesh=mesh,
        in_specs=(tokens_spec,) * 4 + (P(),),
        out_specs=(tokens_spec,) * 3 + (P(("dp", "context"), None),),
        check_vma=False)


def solution(mesh):
    return build(mesh, 8, 8)
```

time: 452 us -> 118 us (0.26)
  waiting for transfers between devices: 345 us -> 0 us
  Pallas kernels: 0 us -> 107 us
  starting transfers between devices: 45.3 us -> 0 us
  matrix products: 19.1 us -> 0 us
  other arithmetic: 14.9 us -> 0 us
  between operations: 14.3 us -> 0.65 us
    unnamed x2 -> x0, waiting for transfers between devices: 264 us -> none
    pallas_call x0 -> x1, Pallas kernels: none -> 107 us  [per_device(): pl.pallas_call(functools.partial(body, sizes), out_shape=(rows, rows, row...]
    all_to_all x4 -> x0, waiting for transfers between devices: 80.6 us -> none  [the longest x1 24.1 us: per_device(): lax.all_to_all(before, 'context', split_axis=0, concat_axis=0, tiled=True)]
    all_to_all x4 -> x0, starting transfers between devices: 45.1 us -> none  [the longest x1 17.1 us: per_device(): lax.all_to_all(kv_groups, 'context', split_axis=0, concat_axis=0, tiled=T...]
    dot_general x18 -> x0, matrix products: 19.1 us -> none  [the longest x3 3.71 us: state_product(): jnp.einsum(form, rows, parts[1], preferred_element_type=jnp.float32)]
    another operation x2 -> x0, other arithmetic: 7.92 us -> none  [the longest x1 6.6 us: block_sums(): running_kv = jnp.cumsum(kv_all, axis=0)]
    reshape x3 -> x0, local copies, waits for them, and re-layouts: 4.75 us -> none  [the longest x1 2.05 us: per_device(): query_heads = queries.reshape(tokens, head_count, head_width)]
  transfers between devices with their start and end apart: 5 -> 0, of which waited for: 5 -> 0; matrix products, arithmetic and copies ran while one was open for 7% -> 0% of each run, Pallas kernels for 0% -> 0%
where the time goes in v1:
time: 118 us; the launch traced here: 116 us
  Pallas kernels  107 us (91%)
  local copies, waits for them, and re-layouts  8.16 us (7%)
    pallas_call x1, Pallas kernels, per_device(): pl.pallas_call(functools.partial(body, sizes), out_shape=(rows, rows, row...  107 us
    unnamed x14, local copies, waits for them, and re-layouts  8.16 us

profile of v1, /device:TPU:1, one launch (start us, length us, event | category | flops | bytes accessed | tf_op | source)
XLA Modules:
  0.0 115.6 jit_solution(16913821640937036898)
XLA Ops:
  0.6 0.0 copy-start
  0.6 1.0 copy-done
  1.7 0.0 copy-start.1
  1.7 1.0 copy-done.1
  2.7 0.0 copy-start.2
  2.7 1.0 copy-done.2
  3.8 0.0 copy-start.3
  3.8 1.0 copy-done.3
  4.8 0.0 copy-start.4
  4.8 1.0 copy-done.4
  5.8 106.8 %shard_map.84 = (bf16[1,128,2048]{2,1,0:T(8,128)(2,1)S(1)}, bf16[1,128,2048]{2,1,0:T(8,128)(2,1)S(1)}, bf16[1,128,2048]{2,1,0:T(8,128)(2,1)S(1)}, f32[4,128]{1,0:T(4,128)S(1)}) custom-call(bf16[1,128,2048]{2,1,0:T(8,128)(2,1)S(1)} %copy-done, bf16[1,128,2048]{2,1,0:T(8,128)(2,1)S(1)} %copy-done.1, bf16[1,128,2048]{2,1,0:T(8,128)(2,1)S(1)} %copy-done.2, ...), custom_call_target="tpu_custom_call" | custom-call | tf_op jit(solution)/shard_map/pallas_call | solution.py:304
  112.6 0.8 copy.13
  113.4 0.8 copy.14
  114.2 0.8 copy.15
  115.0 0.6 copy.16
Async XLA Ops:
  0.6 1.0 copy-start
  1.7 1.0 copy-start.1
  2.7 1.0 copy-start.2
  3.8 1.0 copy-start.3
  4.8 1.0 copy-start.4

commit v2 on v1

--- a/solution.py
+++ b/solution.py
@@ -30,8 +30,9 @@
 
 
 def body(sizes, q_ref, k_ref, v_ref, g_ref, f_ref, qg_ref, kg_ref, vg_ref, mg_ref,
-         a_s, b_s, state, part, base, lda, ldb, lvg, maps, peer, colbuf, rowsum, rowout, rowbuf,
-         part_sem, base_sem, peer_sem, col_sem, row_sem, part_out, base_out, scan_out, peer_out, col_out, row_out):
+         rows_s, maps_s, a_s, b_s, state, part, base, slices, sums, through, lda, ldb, lvg, maps, peer, colbuf, rowsum, rowout, rowbuf,
+         rows_sem, maps_sem, part_sem, base_sem, slice_sem, sum_sem, peer_sem, col_sem, row_sem,
+         part_out, base_out, slice_out, sum_out, peer_out, col_out, row_out):
     ndp, ny, nz, factor, norm = sizes
     tokens, width = q_ref.shape[1], f_ref.shape[1]
     unit = 2 * width
@@ -68,6 +69,27 @@
     for i in range(1, ndp):
         pl.semaphore_signal(barrier, inc=1, **at(lax.rem(d + i, ndp), n))
 
+    def pair_at(m):
+        return pair_of(jnp.where(m == nz - 1, 0, jnp.where(lax.rem(m, 2) == 0, nz - 1 - m // 2, 1 + m // 2)))
+
+    def load(m, carry):
+        p = pair_at(m)
+        for i, ref in enumerate((q_ref, k_ref, v_ref, g_ref)):
+            pltpu.make_async_copy(ref.at[0, :, pl.ds(pl.multiple_of(p * unit, unit), unit)], rows_s.at[p, i], rows_sem.at[p]).start()
+        pltpu.make_async_copy(f_ref.at[pl.ds(2 * p, 2)], maps_s.at[p], maps_sem.at[p]).start()
+        return carry
+
+    lax.fori_loop(0, nz, load, 0)
+
+    def loaded(m, carry):
+        p = pair_at(m)
+        pltpu.make_async_copy(rows_s.at[p], rows_s.at[p], rows_sem.at[p]).wait()
+        pltpu.make_async_copy(maps_s.at[p], maps_s.at[p], maps_sem.at[p]).wait()
+        return carry
+
+    def rows_at(i, p, hh):
+        return rows_s[p, i, :, pl.ds(pl.multiple_of(hh * width, width), width)]
+
     def cols(h):
         return pl.ds(pl.multiple_of(h * width, width), width)
 
@@ -76,23 +98,27 @@
 
     def features(i, carry):
         m, hh = i // 2, lax.rem(i, 2)
-        r = jnp.where(m == nz - 1, 0, jnp.where(lax.rem(m, 2) == 0, nz - 1 - m // 2, 1 + m // 2))
-        p = pair_of(r)
+        p = pair_at(m)
         h = 2 * p + hh
-        fm = f_ref[h]
-        a = nn(q_ref[0, :, cols(h)], fm).astype(BF16)
-        b = nn(k_ref[0, :, cols(h)], fm).astype(BF16)
+        fm = maps_s[p, hh]
+        a = nn(rows_at(0, p, hh), fm).astype(BF16)
+        b = nn(rows_at(1, p, hh), fm).astype(BF16)
         a_s[h] = a
         b_s[h] = b
-        state[0, p, head_rows(hh)] = tn(b, v_ref[0, :, cols(h)])
-        state[1, p, head_rows(hh)] = tn(a, g_ref[0, :, cols(h)])
-        return carry
+        state[0, p, head_rows(hh)] = tn(b, rows_at(2, p, hh))
+        state[1, p, head_rows(hh)] = tn(a, rows_at(3, p, hh))
+        return carry
+
+    def two_pairs(m):
+        lax.fori_loop(m, m + 2, loaded, 0)
+        lax.fori_loop(2 * m, 2 * m + 4, features, 0)
 
     def inside(h, carry):
         causal = (lax.broadcasted_iota(jnp.int32, (tokens, tokens), 0)
                   >= lax.broadcasted_iota(jnp.int32, (tokens, tokens), 1))
         a, b = a_s[h], b_s[h]
-        v, g = v_ref[0, :, cols(h)], g_ref[0, :, cols(h)]
+        p, hh = h // 2, lax.rem(h, 2)
+        v, g = rows_at(2, p, hh), rows_at(3, p, hh)
         sab = jnp.where(causal, nt(a, b), 0.0).astype(BF16)
         sgv = jnp.where(causal, nt(g, v), 0.0).astype(BF16)
         lda[h] = nn(sgv, b)
@@ -113,7 +139,7 @@
     def base_wait(t, j, q):
         base_copy(t, j, q, base.at[t, j, rows_of(q)], n, base_out).wait_recv()
 
-    lax.fori_loop(0, 4, features, 0)
+    two_pairs(0)
     pl.semaphore_wait(barrier, 2 + (ny - 1) + (nz - 1) + (ndp - 1))
     for t in range(2):
         r = nz - 1 if t == 0 else 1
@@ -123,15 +149,16 @@
     def chain(s, carry):
         @pl.when(s <= nz // 2 - 1)
         def _():
-            lax.fori_loop(4 * s, 4 * s + 4, features, 0)
+            two_pairs(2 * s)
 
         @pl.when(s >= nz // 2)
         def _():
             lax.fori_loop(4 * (s - nz // 2), 4 * (s - nz // 2) + 4, inside, 0)
 
-        for q in range(PIECES):
-            for t in range(2):
-                p = pair_of(nz - 1 - s if t == 0 else lax.rem(1 + s, nz))
+        for i in range(2):
+            t = jnp.where(z < nz // 2, 1 - i, i)
+            p = pair_of(jnp.where(t == 0, nz - 1 - s, lax.rem(1 + s, nz)))
+            for q in range(PIECES):
                 part_copy(t, s - 1, q, part.at[t, s - 1, rows_of(q)]).wait_recv()
 
                 @pl.when(order(t) > 0)
@@ -146,37 +173,46 @@
     lax.fori_loop(1, steps + 1, chain, 0)
 
     own = pair_of(0)
-
-    def scan(i, carry):
-        t = jnp.where(y < ny // 2, i, 1 - i)
-        row = jnp.where(t == 0, y, ny - 1 - y)
+    share = unit // ny
+
+    def share_of(row):
+        return pl.ds(pl.multiple_of(row * share, share), share)
+
+    def slice_copy(t, there, source):
+        return pltpu.make_async_remote_copy(
+            src_ref=state.at[t, own, share_of(there)], dst_ref=slices.at[t, source], send_sem=slice_out.at[t],
+            recv_sem=slice_sem.at[t, source], **at(d, there * nz + z))
+
+    def sum_copy(t, there, source):
+        return pltpu.make_async_remote_copy(
+            src_ref=sums.at[t, there], dst_ref=base.at[t, nz - 1, share_of(source)], send_sem=sum_out.at[t],
+            recv_sem=sum_sem.at[t, source], **at(d, there * nz + z))
+
+    for t in range(2):
+        for i in range(1, ny):
+            slice_copy(t, lax.rem(y + i, ny), y).start()
+        slices[t, y] = state[t, own, share_of(y)]
+    for t in range(2):
+        for i in range(1, ny):
+            slice_copy(t, y, lax.rem(y + i, ny)).wait_recv()
+        run = slices[t, 0 if t == 0 else ny - 1]
+        for i in range(1, ny):
+            row = i if t == 0 else ny - 1 - i
+            sums[t, row] = run
+            run = run + slices[t, row]
+        sums[t, 0 if t == 0 else ny - 1] = run
+        for i in range(1, ny):
+            sum_copy(t, lax.rem(y + i, ny), y).start()
+        base[t, nz - 1, share_of(y)] = sums[t, y]
+    for t in range(2):
+        for i in range(1, ny):
+            sum_copy(t, y, lax.rem(y + i, ny)).wait_recv()
+        row = y if t == 0 else ny - 1 - y
         for q in range(PIECES):
-            mine = state.at[t, own, rows_of(q)]
-
-            @pl.when(row > 0)
-            def _(q=q):
-                base_wait(t, nz - 1, q)
-                state[t, own, rows_of(q)] += base[t, nz - 1, rows_of(q)]
-
-            base_copy(t, nz - 1, q, mine, along(t, nz), scan_out).start()
-            base_copy(t, 0, q, mine, along(t, 1), base_out).start()
-
-            @pl.when(row > 0)
-            def _(q=q):
-                base_copy(t, nz - 2, q, base.at[t, nz - 1, rows_of(q)], along(t, -1), base_out).start()
-        return carry
-
-    lax.fori_loop(0, 2, scan, 0)
-
-    def scan_end(i, carry):
-        row = jnp.where(i == 0, y, ny - 1 - y)
-
-        @pl.when(row == 0)
-        def _():
-            for q in range(PIECES):
-                base_wait(i, nz - 1, q)
-                base_copy(i, nz - 2, q, base.at[i, nz - 1, rows_of(q)], along(i, -1), base_out).start()
-        return carry
+            earlier = jnp.where(row > 0, base[t, nz - 1, rows_of(q)], 0.0)
+            through[t, rows_of(q)] = state[t, own, rows_of(q)] + earlier
+            base_copy(t, 0, q, through.at[t, rows_of(q)], along(t, 1), base_out).start()
+            base_copy(t, nz - 2, q, base.at[t, nz - 1, rows_of(q)], along(t, -1), base_out).start()
 
     def state_of(t, j, hh):
         from_base = jnp.where(order(t) >= j, base[t, j - 1, head_rows(hh)], 0.0)
@@ -189,9 +225,8 @@
 
         def finish(hh, carry):
             h = 2 * p + hh
-            q, k = q_ref[0, :, cols(h)], k_ref[0, :, cols(h)]
-            v, g = v_ref[0, :, cols(h)], g_ref[0, :, cols(h)]
-            fm = f_ref[h]
+            q, k, v, g = (rows_at(i, p, hh) for i in range(4))
+            fm = maps_s[p, hh]
             pu, plow = split(state_of(0, nz - r, hh))
             su, sl = split(state_of(1, jnp.where(r == 0, nz, r), hh))
             da = (factor * (lda[h] + (nt(g, pu) + nt(g, plow)))).astype(BF16)
@@ -201,30 +236,31 @@
             qg_ref[0, :, cols(h)] = nt(da, fm).astype(BF16)
             kg_ref[0, :, cols(h)] = nt(db, fm).astype(BF16)
             maps[p, head_rows(hh)] = tn(q, da) + tn(k, db)
+
+            @pl.when(owner != d)
+            def _():
+                pltpu.make_async_remote_copy(
+                    src_ref=maps.at[p, head_rows(hh)], dst_ref=peer.at[place, d, head_rows(hh)], send_sem=peer_out,
+                    recv_sem=peer_sem.at[place, d, hh], **at(owner, n)).start()
             return carry
 
+        owner, place = p // per_owner, lax.rem(p, per_owner)
         lax.fori_loop(0, 2, finish, 0)
-        owner, place = p // per_owner, lax.rem(p, per_owner)
-
-        @pl.when(owner != d)
-        def _():
-            pltpu.make_async_remote_copy(
-                src_ref=maps.at[p], dst_ref=peer.at[place, d], send_sem=peer_out,
-                recv_sem=peer_sem.at[place, d], **at(owner, n)).start()
-
-    lax.fori_loop(0, 2, scan_end, 0)
+
     finish_pair(0)
 
     def spread(hop, carry):
-        for q in range(PIECES):
-            for t in range(2):
+        for i in range(2):
+            t = jnp.where(z < nz // 2, 1 - i, i)
+            other = 1 - t
+            for q in range(PIECES):
                 base_wait(t, hop - 1, q)
                 base_copy(t, hop, q, base.at[t, hop - 1, rows_of(q)], along(t, 1), base_out).start()
-                base_wait(t, nz - 1 - hop, q)
+                base_wait(other, nz - 1 - hop, q)
 
                 @pl.when(hop < left)
-                def _(t=t, q=q):
-                    base_copy(t, nz - 2 - hop, q, base.at[t, nz - 1 - hop, rows_of(q)], along(t, -1), base_out).start()
+                def _(other=other, q=q):
+                    base_copy(other, nz - 2 - hop, q, base.at[other, nz - 1 - hop, rows_of(q)], along(other, -1), base_out).start()
 
         lax.fori_loop(0, 2, lambda i, c: (finish_pair(jnp.where(i == 0, nz - hop, hop)), c)[1], 0)
         return carry
@@ -240,9 +276,11 @@
         rowsum[mine] = maps[d * per_owner + place]
         for i in range(1, ndp):
             source = lax.rem(d + i, ndp)
-            pltpu.make_async_remote_copy(
-                src_ref=maps.at[0], dst_ref=peer.at[place, source], send_sem=peer_out,
-                recv_sem=peer_sem.at[place, source], **at(source, n)).wait_recv()
+            for hh in range(2):
+                half = pl.ds(hh * width, width)
+                pltpu.make_async_remote_copy(
+                    src_ref=maps.at[0, half], dst_ref=peer.at[place, source, half], send_sem=peer_out,
+                    recv_sem=peer_sem.at[place, source, hh], **at(source, n)).wait_recv()
             rowsum[mine] += peer[place, source]
     group = rowsum.shape[0] // ny
     mine = pl.ds(pl.multiple_of(y * group, group), group)
@@ -279,7 +317,8 @@
     for t in range(2):
         sent(part.at[t], part_out.at[t])
         sent(part.at[t], base_out.at[t])
-        sent(state.at[t, 0], scan_out.at[t])
+        sent(slices.at[t, pl.ds(1, ny - 1)], slice_out.at[t])
+        sent(sums.at[t, pl.ds(1, ny - 1)], sum_out.at[t])
     sent(maps.at[pl.ds(0, nz - per_owner)], peer_out)
     sent(colbuf.at[pl.ds(1, ny - 1)], col_out)
     sent(rowbuf.at[pl.ds(1, nz - 1)], row_out)
@@ -304,14 +343,19 @@
         return pl.pallas_call(
             functools.partial(body, sizes),
             out_shape=(rows, rows, rows, jax.ShapeDtypeStruct((small, width), F32)),
-            in_specs=[pl.BlockSpec(memory_space=pltpu.VMEM)] * 5,
+            in_specs=[pl.BlockSpec(memory_space=pl.ANY)] * 5,
             out_specs=(pl.BlockSpec(memory_space=pltpu.VMEM),) * 4,
             scratch_shapes=[
+                pltpu.VMEM((nz, 4, tokens, unit), BF16),
+                pltpu.VMEM((nz, 2, width, width), BF16),
                 pltpu.VMEM((heads, tokens, width), BF16),
                 pltpu.VMEM((heads, tokens, width), BF16),
                 pltpu.VMEM((2, nz, unit, width), F32),
                 pltpu.VMEM((2, nz - 1, unit, width), F32),
                 pltpu.VMEM((2, nz, unit, width), F32),
+                pltpu.VMEM((2, ny, unit // ny, width), F32),
+                pltpu.VMEM((2, ny, unit // ny, width), F32),
+                pltpu.VMEM((2, unit, width), F32),
                 pltpu.VMEM((heads, tokens, width), F32),
                 pltpu.VMEM((heads, tokens, width), F32),
                 pltpu.VMEM((heads, tokens, width), F32),
@@ -321,11 +365,16 @@
                 pltpu.VMEM((owned, width), F32),
                 pltpu.VMEM((nz, small, width), F32),
                 pltpu.VMEM((nz, small, width), F32),
+                dma((nz,)),
+                dma((nz,)),
                 dma((2, nz - 1, PIECES)),
                 dma((2, nz, PIECES)),
-                dma((per_owner, ndp)),
+                dma((2, ny)),
+                dma((2, ny)),
+                dma((per_owner, ndp, 2)),
                 dma((ny,)),
                 dma((nz,)),
+                dma((2,)),
                 dma((2,)),
                 dma((2,)),
                 dma((2,)),
@@ -334,7 +383,7 @@
                 dma(()),
             ],
             compiler_params=pltpu.CompilerParams(
-                collective_id=0, has_side_effects=True, vmem_limit_bytes=48 * 1024 * 1024),
+                collective_id=0, has_side_effects=True, vmem_limit_bytes=62 * 1024 * 1024),
         )(queries, key_rows, value_rows, out_grad, feature_maps)
 
     tokens_spec = P("dp", "context", None)

time: 118 us -> 109 us (0.924); the launches traced: 116 us -> 108 us
  Pallas kernels: 107 us -> 103 us
  local copies, waits for them, and re-layouts: 8.16 us -> 4.55 us
    unnamed x14 -> x10, local copies, waits for them, and re-layouts: 8.16 us -> 4.55 us
    pallas_call x1, Pallas kernels: 107 us -> 103 us  [per_device(): pl.pallas_call(functools.partial(body, sizes), out_shape=(rows, rows, row...]
where the time goes in v2:
time: 109 us; the launch traced here: 108 us
  Pallas kernels  103 us (94%)
  local copies, waits for them, and re-layouts  4.55 us (4%)
    pallas_call x1, Pallas kernels, per_device(): pl.pallas_call(functools.partial(body, sizes), out_shape=(rows, rows, row...  103 us
    unnamed x10, local copies, waits for them, and re-layouts  4.55 us

profile of v2, /device:TPU:1, one launch (start us, length us, event | category | flops | bytes accessed | tf_op | source)
XLA Modules:
  0.0 108.5 jit_solution(9851459650816595221)
XLA Ops:
  0.6 103.3 %shard_map.84 = (bf16[1,128,2048]{2,1,0:T(8,128)(2,1)}, bf16[1,128,2048]{2,1,0:T(8,128)(2,1)}, bf16[1,128,2048]{2,1,0:T(8,128)(2,1)}, f32[4,128]{1,0:T(4,128)}) custom-call(bf16[1,128,2048]{2,1,0:T(8,128)(2,1)} %q_ref.1, bf16[1,128,2048]{2,1,0:T(8,128)(2,1)} %k_ref.1, bf16[1,128,2048]{2,1,0:T(8,128)(2,1)} %v_ref.1, bf16[1,128,2048]{2,1,0:T(8,128)(2,1)} %g_ref.1, ...), custom_call_target="tpu_custom_call" | custom-call | tf_op jit(solution)/shard_map/pallas_call | solution.py:343
  103.9 0.0 copy-start.1
  103.9 1.9 %copy.13 = bf16[1,128,2048]{2,1,0:T(8,128)(2,1)} copy(bf16[1,128,2048]{2,1,0:T(8,128)(2,1)} %get-tuple-element.8) | data formatting | bytes 1048576
  105.8 0.0 copy-done.1
  105.8 0.0 copy-start
  105.8 0.8 copy.14
  106.6 0.4 copy-done
  107.1 0.0 copy-start.2
  107.1 0.8 copy.15
  107.9 0.0 copy-done.2
  107.9 0.6 copy.16
Async XLA Ops:
  103.9 2.0 %copy-start.1 = (bf16[1,128,2048]{2,1,0:T(8,128)(2,1)S(1)}, bf16[1,128,2048]{2,1,0:T(8,128)(2,1)}, u32[]{:S(2)}) copy-start(bf16[1,128,2048]{2,1,0:T(8,128)(2,1)} %get-tuple-element.9) | copy-start | bytes 1572868
  105.8 1.2 %copy-start = (bf16[1,128,2048]{2,1,0:T(8,128)(2,1)S(1)}, bf16[1,128,2048]{2,1,0:T(8,128)(2,1)}, u32[]{:S(2)}) copy-start(bf16[1,128,2048]{2,1,0:T(8,128)(2,1)} %get-tuple-element.10) | copy-start | bytes 1572868
  107.1 0.8 copy-start.2

commit v3 on v2

--- a/solution.py
+++ b/solution.py
@@ -30,14 +30,14 @@
 
 
 def body(sizes, q_ref, k_ref, v_ref, g_ref, f_ref, qg_ref, kg_ref, vg_ref, mg_ref,
-         rows_s, maps_s, a_s, b_s, state, part, base, slices, sums, through, lda, ldb, lvg, maps, peer, colbuf, rowsum, rowout, rowbuf,
-         rows_sem, maps_sem, part_sem, base_sem, slice_sem, sum_sem, peer_sem, col_sem, row_sem,
+         rows_s, maps_s, a_s, b_s, state, part, first, base, slices, sums, through, lda, ldb, lvg, maps, peer, colbuf, rowsum, rowout, rowbuf,
+         rows_sem, maps_sem, part_sem, first_sem, base_sem, slice_sem, sum_sem, peer_sem, col_sem, row_sem,
          part_out, base_out, slice_out, sum_out, peer_out, col_out, row_out):
     ndp, ny, nz, factor, norm = sizes
     tokens, width = q_ref.shape[1], f_ref.shape[1]
     unit = 2 * width
     piece = unit // PIECES
-    steps, right, left = nz - 1, nz // 2, nz // 2 - 1
+    right, left = nz // 2, nz // 2 - 1
     per_owner = nz // ndp
     blocks = ny * nz
     d = lax.axis_index("dp")
@@ -70,7 +70,7 @@
         pl.semaphore_signal(barrier, inc=1, **at(lax.rem(d + i, ndp), n))
 
     def pair_at(m):
-        return pair_of(jnp.where(m == nz - 1, 0, jnp.where(lax.rem(m, 2) == 0, nz - 1 - m // 2, 1 + m // 2)))
+        return pair_of(jnp.where(lax.rem(m, 2) == 0, right + m // 2, left - m // 2))
 
     def load(m, carry):
         p = pair_at(m)
@@ -109,15 +109,16 @@
         state[1, p, head_rows(hh)] = tn(a, rows_at(3, p, hh))
         return carry
 
-    def two_pairs(m):
-        lax.fori_loop(m, m + 2, loaded, 0)
-        lax.fori_loop(2 * m, 2 * m + 4, features, 0)
-
-    def inside(h, carry):
+    def pairs_between(first, last):
+        lax.fori_loop(first, last, loaded, 0)
+        lax.fori_loop(2 * first, 2 * last, features, 0)
+
+    def inside(i, carry):
         causal = (lax.broadcasted_iota(jnp.int32, (tokens, tokens), 0)
                   >= lax.broadcasted_iota(jnp.int32, (tokens, tokens), 1))
+        p, hh = pair_at(i // 2), lax.rem(i, 2)
+        h = 2 * p + hh
         a, b = a_s[h], b_s[h]
-        p, hh = h // 2, lax.rem(h, 2)
         v, g = rows_at(2, p, hh), rows_at(3, p, hh)
         sab = jnp.where(causal, nt(a, b), 0.0).astype(BF16)
         sgv = jnp.where(causal, nt(g, v), 0.0).astype(BF16)
@@ -126,10 +127,32 @@
         lvg[h] = tn(sab, g)
         return carry
 
-    def part_copy(t, s, q, src):
+    def part_copy(t, slot, q, src, target):
         return pltpu.make_async_remote_copy(
-            src_ref=src, dst_ref=part.at[t, s, rows_of(q)], send_sem=part_out.at[t],
-            recv_sem=part_sem.at[t, s, q], **at(d, along(t, 1)))
+            src_ref=src, dst_ref=part.at[t, slot, rows_of(q)], send_sem=part_out.at[t],
+            recv_sem=part_sem.at[t, slot, q], **at(d, target))
+
+    def first_copy(t, q, src, target):
+        return pltpu.make_async_remote_copy(
+            src_ref=src, dst_ref=first.at[t, rows_of(q)], send_sem=part_out.at[t],
+            recv_sem=first_sem.at[t, q], **at(d, target))
+
+    def pair_in(t, r):
+        return pair_of(jnp.where(t == 0, r, nz - r))
+
+    def send_left(t, h, q):
+        src = state.at[t, pair_in(t, right + h), rows_of(q)]
+
+        @pl.when(order(t) > 0)
+        def _():
+            part_copy(t, h, q, src, along(t, -1)).start()
+
+        @pl.when(order(t) == 0)
+        def _():
+            first_copy(t, q, src, along(t, right + h)).start()
+
+    def send_right(t, h, q):
+        part_copy(t, right + h, q, state.at[t, pair_in(t, left - h), rows_of(q)], along(t, 1)).start()
 
     def base_copy(t, j, q, src, target, sem):
         return pltpu.make_async_remote_copy(
@@ -139,40 +162,58 @@
     def base_wait(t, j, q):
         base_copy(t, j, q, base.at[t, j, rows_of(q)], n, base_out).wait_recv()
 
-    two_pairs(0)
+    pairs_between(0, 3)
     pl.semaphore_wait(barrier, 2 + (ny - 1) + (nz - 1) + (ndp - 1))
-    for t in range(2):
-        r = nz - 1 if t == 0 else 1
-        for q in range(PIECES):
-            part_copy(t, 0, q, state.at[t, pair_of(r), rows_of(q)]).start()
-
-    def chain(s, carry):
-        @pl.when(s <= nz // 2 - 1)
-        def _():
-            two_pairs(2 * s)
-
-        @pl.when(s >= nz // 2)
-        def _():
-            lax.fori_loop(4 * (s - nz // 2), 4 * (s - nz // 2) + 4, inside, 0)
-
+    for q in range(PIECES):
+        for t in range(2):
+            send_left(t, 0, q)
+    for q in range(PIECES):
+        for t in range(2):
+            send_right(t, 0, q)
+
+    def chain(h, carry):
+        pairs_between(jnp.minimum(1 + 2 * h, nz), jnp.minimum(3 + 2 * h, nz))
+        lax.fori_loop(4 * (h - 1), 4 * h, inside, 0)
         for i in range(2):
-            t = jnp.where(z < nz // 2, 1 - i, i)
-            p = pair_of(jnp.where(t == 0, nz - 1 - s, lax.rem(1 + s, nz)))
+            t = jnp.where(z < nz // 2, i, 1 - i)
             for q in range(PIECES):
-                part_copy(t, s - 1, q, part.at[t, s - 1, rows_of(q)]).wait_recv()
-
-                @pl.when(order(t) > 0)
+                p = pair_in(t, lax.rem(right + h, nz))
+
+                @pl.when(order(t) < blocks - 1)
                 def _(t=t, p=p, q=q):
-                    state[t, p, rows_of(q)] += part[t, s - 1, rows_of(q)]
-
-                @pl.when(s < steps)
-                def _(t=t, p=p, q=q):
-                    part_copy(t, s, q, state.at[t, p, rows_of(q)]).start()
-        return carry
-
-    lax.fori_loop(1, steps + 1, chain, 0)
-
+                    part_copy(t, h - 1, q, part.at[t, h - 1, rows_of(q)], n).wait_recv()
+                    state[t, p, rows_of(q)] += part[t, h - 1, rows_of(q)]
+
+                @pl.when(h < right)
+                def _(t=t, q=q):
+                    send_left(t, h, q)
+
+            other = 1 - t
+
+            @pl.when(h <= left)
+            def _(other=other):
+                for q in range(PIECES):
+                    p = pair_in(other, left - h)
+                    part_copy(other, right + h - 1, q, part.at[other, right + h - 1, rows_of(q)], n).wait_recv()
+
+                    @pl.when(order(other) > 0)
+                    def _(p=p, q=q):
+                        state[other, p, rows_of(q)] += part[other, right + h - 1, rows_of(q)]
+
+                    @pl.when(h < left)
+                    def _(q=q):
+                        send_right(other, h, q)
+        return carry
+
+    lax.fori_loop(1, right + 1, chain, 0)
     own = pair_of(0)
+    for t in range(2):
+        @pl.when(jnp.logical_and(order(t) >= right, order(t) < nz))
+        def _(t=t):
+            for q in range(PIECES):
+                first_copy(t, q, first.at[t, rows_of(q)], n).wait_recv()
+                state[t, own, rows_of(q)] += first[t, rows_of(q)]
+
     share = unit // ny
 
     def share_of(row):
@@ -212,13 +253,20 @@
             earlier = jnp.where(row > 0, base[t, nz - 1, rows_of(q)], 0.0)
             through[t, rows_of(q)] = state[t, own, rows_of(q)] + earlier
             base_copy(t, 0, q, through.at[t, rows_of(q)], along(t, 1), base_out).start()
+
+            @pl.when(jnp.logical_and(order(t) >= right, order(t) < nz))
+            def _(t=t, q=q):
+                base[t, nz - 1, rows_of(q)] = first[t, rows_of(q)]
+
             base_copy(t, nz - 2, q, base.at[t, nz - 1, rows_of(q)], along(t, -1), base_out).start()
 
-    def state_of(t, j, hh):
-        from_base = jnp.where(order(t) >= j, base[t, j - 1, head_rows(hh)], 0.0)
-        has_part = jnp.logical_and(order(t) > 0, j >= 2)
-        slot = jnp.maximum(j - 2, 0)
-        return from_base + jnp.where(has_part, part[t, slot, head_rows(hh)], 0.0)
+    def state_of(t, p, r, hh):
+        given = base[t, nz - 1 - r, head_rows(hh)]
+        ahead = jnp.where(order(t) > 0, given - state[t, p, head_rows(hh)], 0.0)
+        chained = part[t, right + jnp.maximum(left - 1 - r, 0), head_rows(hh)]
+        has_chained = jnp.logical_and(order(t) > 0, r < left)
+        behind = jnp.where(order(t) + r >= right, given, 0.0) + jnp.where(has_chained, chained, 0.0)
+        return jnp.where(r >= right, ahead, behind)
 
     def finish_pair(r):
         p = pair_of(r)
@@ -227,8 +275,8 @@
             h = 2 * p + hh
             q, k, v, g = (rows_at(i, p, hh) for i in range(4))
             fm = maps_s[p, hh]
-            pu, plow = split(state_of(0, nz - r, hh))
-            su, sl = split(state_of(1, jnp.where(r == 0, nz, r), hh))
+            pu, plow = split(state_of(0, p, r, hh))
+            su, sl = split(state_of(1, p, lax.rem(nz - r, nz), hh))
             da = (factor * (lda[h] + (nt(g, pu) + nt(g, plow)))).astype(BF16)
             db = (factor * (ldb[h] + (nt(v, su) + nt(v, sl)))).astype(BF16)
             b = b_s[h]
@@ -247,7 +295,7 @@
         owner, place = p // per_owner, lax.rem(p, per_owner)
         lax.fori_loop(0, 2, finish, 0)
 
-    finish_pair(0)
+    finish_pair(jnp.int32(0))
 
     def spread(hop, carry):
         for i in range(2):
@@ -255,7 +303,15 @@
             other = 1 - t
             for q in range(PIECES):
                 base_wait(t, hop - 1, q)
-                base_copy(t, hop, q, base.at[t, hop - 1, rows_of(q)], along(t, 1), base_out).start()
+
+                @pl.when(order(t) > 0)
+                def _(t=t, q=q):
+                    base_copy(t, hop, q, base.at[t, hop - 1, rows_of(q)], along(t, 1), base_out).start()
+
+                @pl.when(order(t) == 0)
+                def _(t=t, q=q):
+                    base_copy(t, hop, q, state.at[t, pair_in(t, nz - hop), rows_of(q)], along(t, 1), base_out).start()
+
                 base_wait(other, nz - 1 - hop, q)
 
                 @pl.when(hop < left)
@@ -324,6 +380,15 @@
     sent(rowbuf.at[pl.ds(1, nz - 1)], row_out)
 
 
+def write_out(*refs):
+    sems = refs[8]
+    copies = [pltpu.make_async_copy(refs[i], refs[4 + i], sems.at[i]) for i in range(4)]
+    for copy in copies:
+        copy.start()
+    for copy in copies:
+        copy.wait()
+
+
 def build(mesh, ny, nz):
     ndp = mesh.shape["dp"]
 
@@ -340,10 +405,10 @@
         sizes = (ndp, ny, nz, 1.0 / math.sqrt(width * length), 1.0 / math.sqrt(ndp * length))
         dma = pltpu.SemaphoreType.DMA
         rows = jax.ShapeDtypeStruct(queries.shape, BF16)
-        return pl.pallas_call(
+        results = pl.pallas_call(
             functools.partial(body, sizes),
             out_shape=(rows, rows, rows, jax.ShapeDtypeStruct((small, width), F32)),
-            in_specs=[pl.BlockSpec(memory_space=pl.ANY)] * 5,
+            in_specs=[pl.BlockSpec(memory_space=pltpu.HBM)] * 5,
             out_specs=(pl.BlockSpec(memory_space=pltpu.VMEM),) * 4,
             scratch_shapes=[
                 pltpu.VMEM((nz, 4, tokens, unit), BF16),
@@ -352,6 +417,7 @@
                 pltpu.VMEM((heads, tokens, width), BF16),
                 pltpu.VMEM((2, nz, unit, width), F32),
                 pltpu.VMEM((2, nz - 1, unit, width), F32),
+                pltpu.VMEM((2, unit, width), F32),
                 pltpu.VMEM((2, nz, unit, width), F32),
                 pltpu.VMEM((2, ny, unit // ny, width), F32),
                 pltpu.VMEM((2, ny, unit // ny, width), F32),
@@ -368,6 +434,7 @@
                 dma((nz,)),
                 dma((nz,)),
                 dma((2, nz - 1, PIECES)),
+                dma((2, PIECES)),
                 dma((2, nz, PIECES)),
                 dma((2, ny)),
                 dma((2, ny)),
@@ -385,6 +452,13 @@
             compiler_params=pltpu.CompilerParams(
                 collective_id=0, has_side_effects=True, vmem_limit_bytes=62 * 1024 * 1024),
         )(queries, key_rows, value_rows, out_grad, feature_maps)
+        return pl.pallas_call(
+            write_out,
+            out_shape=tuple(jax.ShapeDtypeStruct(x.shape, x.dtype) for x in results),
+            in_specs=[pl.BlockSpec(memory_space=pltpu.VMEM)] * 4,
+            out_specs=(pl.BlockSpec(memory_space=pltpu.HBM),) * 4,
+            scratch_shapes=[dma((4,))],
+        )(*results)
 
     tokens_spec = P("dp", "context", None)
     return jax.shard_map(

time: 109 us -> 99.6 us (0.914)
  local copies, waits for them, and re-layouts: 4.55 us -> 0 us
  Pallas kernels: 103 us -> 98.8 us
    pallas_call x1, Pallas kernels: 103 us -> 96.2 us  [per_device(): pl.pallas_call(functools.partial(body, sizes), out_shape=(rows, rows, row...]
    unnamed x10 -> x0, local copies, waits for them, and re-layouts: 4.55 us -> none
    pallas_call x0 -> x1, Pallas kernels: none -> 2.54 us  [per_device(): pl.pallas_call(write_out, out_shape=tuple((jax.ShapeDtypeStruct(x.shape,...]
where the time goes in v3:
time: 99.6 us; the launch traced here: 99.4 us
  Pallas kernels  98.8 us (99%)
    pallas_call x1, Pallas kernels, per_device(): pl.pallas_call(functools.partial(body, sizes), out_shape=(rows, rows, row...  96.2 us
    pallas_call x1, Pallas kernels, per_device(): pl.pallas_call(write_out, out_shape=tuple((jax.ShapeDtypeStruct(x.shape,...  2.54 us

profile of v3, /device:TPU:1, one launch (start us, length us, event | category | flops | bytes accessed | tf_op | source)
XLA Modules:
  0.0 99.4 jit_solution(18064617600191031249)
XLA Ops:
  0.6 96.2 %shard_map.84 = (bf16[1,128,2048]{2,1,0:T(8,128)(2,1)}, bf16[1,128,2048]{2,1,0:T(8,128)(2,1)}, bf16[1,128,2048]{2,1,0:T(8,128)(2,1)}, f32[4,128]{1,0:T(4,128)}) custom-call(bf16[1,128,2048]{2,1,0:T(8,128)(2,1)} %q_ref.1, bf16[1,128,2048]{2,1,0:T(8,128)(2,1)} %k_ref.1, bf16[1,128,2048]{2,1,0:T(8,128)(2,1)} %v_ref.1, bf16[1,128,2048]{2,1,0:T(8,128)(2,1)} %g_ref.1, ...), custom_call_target="tpu_custom_call" | custom-call | tf_op jit(solution)/shard_map/pallas_call | solution.py:408
  96.9 2.5 %shard_map.85 = (bf16[1,128,2048]{2,1,0:T(8,128)(2,1)}, bf16[1,128,2048]{2,1,0:T(8,128)(2,1)}, bf16[1,128,2048]{2,1,0:T(8,128)(2,1)}, f32[4,128]{1,0:T(4,128)}) custom-call(bf16[1,128,2048]{2,1,0:T(8,128)(2,1)} %get-tuple-element.8.refs_0_, bf16[1,128,2048]{2,1,0:T(8,128)(2,1)} %get-tuple-element.9.refs_1_, bf16[1,128,2048]{2,1,0:T(8,128)(2,1)} %get-tuple-element.10.refs_2_, ...), custom_call_target="tpu_custom_call" | custom-call | tf_op jit(solution)/shard_map/pallas_call | solution.py:455

commit v4 on v3

--- a/solution.py
+++ b/solution.py
@@ -10,6 +10,7 @@
 
 F32, BF16 = jnp.float32, jnp.bfloat16
 PIECES = 2
+BANDS = 4
 
 
 def nn(a, b):
@@ -30,9 +31,9 @@
 
 
 def body(sizes, q_ref, k_ref, v_ref, g_ref, f_ref, qg_ref, kg_ref, vg_ref, mg_ref,
-         rows_s, maps_s, a_s, b_s, state, part, first, base, slices, sums, through, lda, ldb, lvg, maps, peer, colbuf, rowsum, rowout, rowbuf,
+         rows_s, maps_s, a_s, b_s, state, part, first, base, slices, sums, through, lda, ldb, lvg, maps, peer, colbuf, rowsum, rowout, rowbuf, da_s, db_s, out_s,
          rows_sem, maps_sem, part_sem, first_sem, base_sem, slice_sem, sum_sem, peer_sem, col_sem, row_sem,
-         part_out, base_out, slice_out, sum_out, peer_out, col_out, row_out):
+         part_out, base_out, slice_out, sum_out, peer_out, col_out, row_out, out_sem):
     ndp, ny, nz, factor, norm = sizes
     tokens, width = q_ref.shape[1], f_ref.shape[1]
     unit = 2 * width
@@ -162,11 +163,12 @@
     def base_wait(t, j, q):
         base_copy(t, j, q, base.at[t, j, rows_of(q)], n, base_out).wait_recv()
 
-    pairs_between(0, 3)
+    pairs_between(0, 1)
     pl.semaphore_wait(barrier, 2 + (ny - 1) + (nz - 1) + (ndp - 1))
     for q in range(PIECES):
         for t in range(2):
             send_left(t, 0, q)
+    pairs_between(1, 3)
     for q in range(PIECES):
         for t in range(2):
             send_right(t, 0, q)
@@ -271,18 +273,15 @@
     def finish_pair(r):
         p = pair_of(r)
 
-        def finish(hh, carry):
+        def gradients(hh, carry):
             h = 2 * p + hh
             q, k, v, g = (rows_at(i, p, hh) for i in range(4))
-            fm = maps_s[p, hh]
             pu, plow = split(state_of(0, p, r, hh))
             su, sl = split(state_of(1, p, lax.rem(nz - r, nz), hh))
             da = (factor * (lda[h] + (nt(g, pu) + nt(g, plow)))).astype(BF16)
             db = (factor * (ldb[h] + (nt(v, su) + nt(v, sl)))).astype(BF16)
-            b = b_s[h]
-            vg_ref[0, :, cols(h)] = (factor * (lvg[h] + (nn(b, su) + nn(b, sl)))).astype(BF16)
-            qg_ref[0, :, cols(h)] = nt(da, fm).astype(BF16)
-            kg_ref[0, :, cols(h)] = nt(db, fm).astype(BF16)
+            da_s[hh] = da
+            db_s[hh] = db
             maps[p, head_rows(hh)] = tn(q, da) + tn(k, db)
 
             @pl.when(owner != d)
@@ -292,8 +291,22 @@
                     recv_sem=peer_sem.at[place, d, hh], **at(owner, n)).start()
             return carry
 
+        def outputs(hh, carry):
+            h = 2 * p + hh
+            fm = maps_s[p, hh]
+            su, sl = split(state_of(1, p, lax.rem(nz - r, nz), hh))
+            b = b_s[h]
+            mine = pl.ds(pl.multiple_of(hh * width, width), width)
+            out_s[p, 0, :, mine] = nt(da_s[hh], fm).astype(BF16)
+            out_s[p, 1, :, mine] = nt(db_s[hh], fm).astype(BF16)
+            out_s[p, 2, :, mine] = (factor * (lvg[h] + (nn(b, su) + nn(b, sl)))).astype(BF16)
+            return carry
+
         owner, place = p // per_owner, lax.rem(p, per_owner)
-        lax.fori_loop(0, 2, finish, 0)
+        lax.fori_loop(0, 2, gradients, 0)
+        lax.fori_loop(0, 2, outputs, 0)
+        for i, ref in enumerate((qg_ref, kg_ref, vg_ref)):
+            pltpu.make_async_copy(out_s.at[p, i], ref.at[0, :, pl.ds(pl.multiple_of(p * unit, unit), unit)], out_sem).start()
 
     finish_pair(jnp.int32(0))
 
@@ -367,6 +380,8 @@
         last = last + rowbuf[i]
     mg_ref[...] = last * norm
 
+    pltpu.make_async_copy(out_s, out_s, out_sem).wait()
+
     def sent(ref, sem):
         pltpu.make_async_remote_copy(src_ref=ref, dst_ref=ref, send_sem=sem, recv_sem=row_sem.at[0], **at(d, n)).wait_send()
 
@@ -381,11 +396,19 @@
 
 
 def write_out(*refs):
-    sems = refs[8]
-    copies = [pltpu.make_async_copy(refs[i], refs[4 + i], sems.at[i]) for i in range(4)]
-    for copy in copies:
+    held, small, in_sem, out_sem = refs[8:]
+    rows = held.shape[1] // BANDS
+    bands = [(i, pl.ds(j * rows, rows), i * BANDS + j) for i in range(3) for j in range(BANDS)]
+    fetch = [pltpu.make_async_copy(refs[i].at[0, band], held.at[i, band], in_sem.at[k]) for i, band, k in bands]
+    store = [pltpu.make_async_copy(held.at[i, band], refs[4 + i].at[0, band], out_sem.at[k]) for i, band, k in bands]
+    fetch.append(pltpu.make_async_copy(refs[3], small, in_sem.at[3 * BANDS]))
+    store.append(pltpu.make_async_copy(small, refs[7], out_sem.at[3 * BANDS]))
+    for copy in fetch:
         copy.start()
-    for copy in copies:
+    for arrived, copy in zip(fetch, store):
+        arrived.wait()
+        copy.start()
+    for copy in store:
         copy.wait()
 
 
@@ -408,8 +431,8 @@
         results = pl.pallas_call(
             functools.partial(body, sizes),
             out_shape=(rows, rows, rows, jax.ShapeDtypeStruct((small, width), F32)),
-            in_specs=[pl.BlockSpec(memory_space=pltpu.HBM)] * 5,
-            out_specs=(pl.BlockSpec(memory_space=pltpu.VMEM),) * 4,
+            in_specs=[pl.BlockSpec(memory_space=pl.ANY)] * 5,
+            out_specs=(pl.BlockSpec(memory_space=pl.ANY),) * 3 + (pl.BlockSpec(memory_space=pltpu.VMEM),),
             scratch_shapes=[
                 pltpu.VMEM((nz, 4, tokens, unit), BF16),
                 pltpu.VMEM((nz, 2, width, width), BF16),
@@ -431,6 +454,9 @@
                 pltpu.VMEM((owned, width), F32),
                 pltpu.VMEM((nz, small, width), F32),
                 pltpu.VMEM((nz, small, width), F32),
+                pltpu.VMEM((2, tokens, width), BF16),
+                pltpu.VMEM((2, tokens, width), BF16),
+                pltpu.VMEM((nz, 3, tokens, unit), BF16),
                 dma((nz,)),
                 dma((nz,)),
                 dma((2, nz - 1, PIECES)),
@@ -448,6 +474,7 @@
                 dma(()),
                 dma(()),
                 dma(()),
+                dma(()),
             ],
             compiler_params=pltpu.CompilerParams(
                 collective_id=0, has_side_effects=True, vmem_limit_bytes=62 * 1024 * 1024),
@@ -455,9 +482,15 @@
         return pl.pallas_call(
             write_out,
             out_shape=tuple(jax.ShapeDtypeStruct(x.shape, x.dtype) for x in results),
-            in_specs=[pl.BlockSpec(memory_space=pltpu.VMEM)] * 4,
-            out_specs=(pl.BlockSpec(memory_space=pltpu.HBM),) * 4,
-            scratch_shapes=[dma((4,))],
+            in_specs=[pl.BlockSpec(memory_space=pl.ANY)] * 4,
+            out_specs=(pl.BlockSpec(memory_space=pl.ANY),) * 4,
+            scratch_shapes=[
+                pltpu.VMEM((3,) + queries.shape[1:], BF16),
+                pltpu.VMEM((small, width), F32),
+                dma((3 * BANDS + 1,)),
+                dma((3 * BANDS + 1,)),
+            ],
+            compiler_params=pltpu.CompilerParams(vmem_limit_bytes=62 * 1024 * 1024),
         )(*results)
 
     tokens_spec = P("dp", "context", None)

time: 99.6 us -> 97.6 us (0.980)
  Pallas kernels: 98.8 us -> 96.8 us
    pallas_call x1, Pallas kernels: 96.2 us -> 94.4 us  [per_device(): pl.pallas_call(functools.partial(body, sizes), out_shape=(rows, rows, row...]
where the time goes in v4:
time: 97.6 us; the launch traced here: 97.4 us
  Pallas kernels  96.8 us (99%)
    pallas_call x1, Pallas kernels, per_device(): pl.pallas_call(functools.partial(body, sizes), out_shape=(rows, rows, row...  94.4 us
    pallas_call x1, Pallas kernels, per_device(): pl.pallas_call(write_out, out_shape=tuple((jax.ShapeDtypeStruct(x.shape,...  2.35 us

profile of v4, /device:TPU:1, one launch (start us, length us, event | category | flops | bytes accessed | tf_op | source)
XLA Modules:
  0.0 97.4 jit_solution(18085694852209816997)
XLA Ops:
  0.6 94.4 %shard_map.84 = (bf16[1,128,2048]{2,1,0:T(8,128)(2,1)}, bf16[1,128,2048]{2,1,0:T(8,128)(2,1)}, bf16[1,128,2048]{2,1,0:T(8,128)(2,1)}, f32[4,128]{1,0:T(4,128)}) custom-call(bf16[1,128,2048]{2,1,0:T(8,128)(2,1)} %q_ref.1, bf16[1,128,2048]{2,1,0:T(8,128)(2,1)} %k_ref.1, bf16[1,128,2048]{2,1,0:T(8,128)(2,1)} %v_ref.1, bf16[1,128,2048]{2,1,0:T(8,128)(2,1)} %g_ref.1, ...), custom_call_target="tpu_custom_call" | custom-call | tf_op jit(solution)/shard_map/pallas_call | solution.py:431
  95.1 2.3 %shard_map.85 = (bf16[1,128,2048]{2,1,0:T(8,128)(2,1)}, bf16[1,128,2048]{2,1,0:T(8,128)(2,1)}, bf16[1,128,2048]{2,1,0:T(8,128)(2,1)}, f32[4,128]{1,0:T(4,128)}) custom-call(bf16[1,128,2048]{2,1,0:T(8,128)(2,1)} %get-tuple-element.8.refs_0_, bf16[1,128,2048]{2,1,0:T(8,128)(2,1)} %get-tuple-element.9.refs_1_, bf16[1,128,2048]{2,1,0:T(8,128)(2,1)} %get-tuple-element.10.refs_2_, ...), custom_call_target="tpu_custom_call" | custom-call | tf_op jit(solution)/shard_map/pallas_call | solution.py:482

commit v5 on v4

--- a/solution.py
+++ b/solution.py
@@ -9,7 +9,7 @@
 from jax.sharding import PartitionSpec as P
 
 F32, BF16 = jnp.float32, jnp.bfloat16
-PIECES = 2
+PIECES = 1
 BANDS = 4
 
 
@@ -231,8 +231,9 @@
             src_ref=sums.at[t, there], dst_ref=base.at[t, nz - 1, share_of(source)], send_sem=sum_out.at[t],
             recv_sem=sum_sem.at[t, source], **at(d, there * nz + z))
 
+    far_first = sorted(range(1, ny), key=lambda i: -min(i, ny - i))
     for t in range(2):
-        for i in range(1, ny):
+        for i in far_first:
             slice_copy(t, lax.rem(y + i, ny), y).start()
         slices[t, y] = state[t, own, share_of(y)]
     for t in range(2):
@@ -244,14 +245,17 @@
             sums[t, row] = run
             run = run + slices[t, row]
         sums[t, 0 if t == 0 else ny - 1] = run
-        for i in range(1, ny):
+        for i in far_first:
             sum_copy(t, lax.rem(y + i, ny), y).start()
         base[t, nz - 1, share_of(y)] = sums[t, y]
     for t in range(2):
-        for i in range(1, ny):
-            sum_copy(t, y, lax.rem(y + i, ny)).wait_recv()
         row = y if t == 0 else ny - 1 - y
         for q in range(PIECES):
+            for source in range(q * ny // PIECES, (q + 1) * ny // PIECES):
+                @pl.when(source != y)
+                def _(t=t, source=source):
+                    sum_copy(t, y, source).wait_recv()
+
             earlier = jnp.where(row > 0, base[t, nz - 1, rows_of(q)], 0.0)
             through[t, rows_of(q)] = state[t, own, rows_of(q)] + earlier
             base_copy(t, 0, q, through.at[t, rows_of(q)], along(t, 1), base_out).start()
@@ -353,7 +357,7 @@
             rowsum[mine] += peer[place, source]
     group = rowsum.shape[0] // ny
     mine = pl.ds(pl.multiple_of(y * group, group), group)
-    for i in range(1, ny):
+    for i in far_first:
         there = lax.rem(y + i, ny)
         pltpu.make_async_remote_copy(
             src_ref=rowsum.at[pl.ds(pl.multiple_of(there * group, group), group)], dst_ref=colbuf.at[i], send_sem=col_out,
@@ -367,7 +371,7 @@
     small = group // nz
     for i in range(nz):
         rowout[i] = total[i * small:(i + 1) * small]
-    for i in range(1, nz):
+    for i in sorted(range(1, nz), key=lambda i: -min(i, nz - i)):
         there = lax.rem(z + i, nz)
         pltpu.make_async_remote_copy(
             src_ref=rowout.at[there], dst_ref=rowbuf.at[i], send_sem=row_out,

time: 97.6 us -> 96.2 us (0.986)
  Pallas kernels: 96.8 us -> 95.4 us
    pallas_call x1, Pallas kernels: 94.4 us -> 93 us  [per_device(): pl.pallas_call(functools.partial(body, sizes), out_shape=(rows, rows, row...]
where the time goes in v5:
time: 96.2 us; the launch traced here: 96 us
  Pallas kernels  95.4 us (99%)
    pallas_call x1, Pallas kernels, per_device(): pl.pallas_call(functools.partial(body, sizes), out_shape=(rows, rows, row...  93 us
    pallas_call x1, Pallas kernels, per_device(): pl.pallas_call(write_out, out_shape=tuple((jax.ShapeDtypeStruct(x.shape,...  2.35 us

profile of v5, /device:TPU:1, one launch (start us, length us, event | category | flops | bytes accessed | tf_op | source)
XLA Modules:
  0.0 96.0 jit_solution(4789636142057096849)
XLA Ops:
  0.6 93.0 %shard_map.84 = (bf16[1,128,2048]{2,1,0:T(8,128)(2,1)}, bf16[1,128,2048]{2,1,0:T(8,128)(2,1)}, bf16[1,128,2048]{2,1,0:T(8,128)(2,1)}, f32[4,128]{1,0:T(4,128)}) custom-call(bf16[1,128,2048]{2,1,0:T(8,128)(2,1)} %q_ref.1, bf16[1,128,2048]{2,1,0:T(8,128)(2,1)} %k_ref.1, bf16[1,128,2048]{2,1,0:T(8,128)(2,1)} %v_ref.1, bf16[1,128,2048]{2,1,0:T(8,128)(2,1)} %g_ref.1, ...), custom_call_target="tpu_custom_call" | custom-call | tf_op jit(solution)/shard_map/pallas_call | solution.py:435
  93.7 2.3 %shard_map.85 = (bf16[1,128,2048]{2,1,0:T(8,128)(2,1)}, bf16[1,128,2048]{2,1,0:T(8,128)(2,1)}, bf16[1,128,2048]{2,1,0:T(8,128)(2,1)}, f32[4,128]{1,0:T(4,128)}) custom-call(bf16[1,128,2048]{2,1,0:T(8,128)(2,1)} %get-tuple-element.8.refs_0_, bf16[1,128,2048]{2,1,0:T(8,128)(2,1)} %get-tuple-element.9.refs_1_, bf16[1,128,2048]{2,1,0:T(8,128)(2,1)} %get-tuple-element.10.refs_2_, ...), custom_call_target="tpu_custom_call" | custom-call | tf_op jit(solution)/shard_map/pallas_call | solution.py:486
